TPU v7x, 512 devices: a whole 4x8x8 slice. The times are simulated.
512 devices in a mesh: pts: 32 (over z_lo, y, core), ctr: 16 (over z_hi, x).
Axes of the slice: x: 4, y: 8, z: 8 (z_hi: 4, z_lo: 2; z = z_hi * 2 + z_lo), core: 2. Of those that a mesh axis runs over, the one named last changes fastest.
Arguments:
- points: bfloat16 [8192, 256], P('pts', 'ctr'), may hold values from -6 to 6
- centres: bfloat16 [8192, 256], P('ctr', 'pts'), may hold values from -6 to 6
- precisions: float32 [256], replicated, may hold values from 9.765625e-05 to 0.01953125
- targets: bfloat16 [8192, 128], P('pts', 'ctr'), may hold values from -6 to 6
Outputs:
- coefficients: float32 [8192, 128], P('ctr')
- residual: float32 [8192, 128], P('ctr')
All inputs are finite; a program needn't handle non-finite values.
Results may differ from a plain program's by a relative error of at most 0.0033.
Values may be sent and summed in bfloat16 or wider, within the bound.
No kernel may reach another device: no remote copies, remote signals or barrier semaphores. Data moves between devices by JAX's collectives and lax.ppermute only.
A program may use at most 64 MiB of HBM per device.

v0:
```python
import math
import jax
import jax.numpy as jnp
from jax import lax
from jax.sharding import PartitionSpec as P

FEATURES = 256
BLOCK = 512
NEWTON = 2
ridge_weight = 0.05
jitter_term = 0.1
highest = lax.Precision.HIGHEST


def block_product(matrices, vectors):
    grouped = vectors.reshape(matrices.shape[0], matrices.shape[1], vectors.shape[1])
    return jnp.einsum("bij,bjr->bir", matrices, grouped, precision=highest).reshape(vectors.shape)


def batched(left, right):
    return jnp.einsum("bij,bjk->bik", left, right, precision=highest)


def on_device(points, centres, precisions, targets):
    full_points, full_targets = (
        lax.all_gather(points, "ctr", axis=1, tiled=True),
        lax.all_gather(targets, "ctr", axis=1, tiled=True),
    )
    full_centres = lax.all_gather(centres, "pts", axis=1, tiled=True)
    total = points.shape[0] * lax.axis_size("pts")
    count_blocks = centres.shape[0] // BLOCK
    point_float = full_points.astype(jnp.float32)
    point_square = jnp.sum(precisions * point_float * point_float, axis=1)
    scaled_points = (point_float * precisions).astype(jnp.bfloat16)
    centre_float = full_centres.astype(jnp.float32)
    centre_square = jnp.sum(precisions * centre_float * centre_float, axis=1)
    scaled_centres = (centre_float * precisions).astype(jnp.bfloat16)
    cross_term = lax.dot_general(
        scaled_points, full_centres, (((1,), (1,)), ((), ())), preferred_element_type=jnp.float32
    )
    kernel_tile = jnp.exp(-(point_square[:, None] + centre_square[None, :] - 2.0 * cross_term))
    grouped_scaled = scaled_centres.reshape(count_blocks, BLOCK, FEATURES)
    grouped_centres = full_centres.reshape(count_blocks, BLOCK, FEATURES)
    block_cross = jnp.einsum(
        "bif,bjf->bij", grouped_scaled, grouped_centres, preferred_element_type=jnp.float32
    )
    grouped_square = centre_square.reshape(count_blocks, BLOCK)
    similar = jnp.exp(
        -(grouped_square[:, :, None] + grouped_square[:, None, :] - 2.0 * block_cross)
    )
    identity = jnp.eye(BLOCK, dtype=jnp.float32)
    blocks = 0.5 * (similar + jnp.swapaxes(similar, 1, 2)) + jitter_term * identity
    scale = jnp.sqrt(jnp.sum(blocks * blocks, axis=(1, 2)))
    current_y = blocks / scale[:, None, None]
    current_z = jnp.broadcast_to(identity, blocks.shape)
    width = BLOCK // lax.axis_size("pts")
    first = lax.axis_index("pts") * width
    rows_iota = lax.broadcasted_iota(jnp.int32, (BLOCK, width), 0)
    cols_iota = lax.broadcasted_iota(jnp.int32, (BLOCK, width), 1)
    identity_cols = jnp.where(rows_iota == cols_iota + first, 1.0, 0.0).astype(jnp.float32)
    for newton_step in range(NEWTON):
        y_columns = lax.dynamic_slice_in_dim(current_y, first, width, 2)
        factor = 3.0 * identity_cols - batched(current_z, y_columns)
        next_y = 0.5 * batched(current_y, factor)
        next_z = 0.5 * batched(current_z, factor)
        if newton_step + 1 < NEWTON:
            current_y, current_z = (
                lax.all_gather(next_y, "pts", axis=2, tiled=True),
                lax.all_gather(next_z, "pts", axis=2, tiled=True),
            )
        else:
            current_z = lax.all_gather(next_z, "pts", axis=2, tiled=True)
    target_float = full_targets.astype(jnp.float32)
    right_part = lax.dot_general(
        kernel_tile, target_float, (((0,), (0,)), ((), ())), precision=highest
    )
    right = lax.psum(right_part, "pts") / math.sqrt(total)
    gradient = block_product(current_z, right)
    residual = gradient
    direction = residual
    norm_now = lax.psum(jnp.sum(residual * residual, axis=0), "ctr")
    spread = block_product(current_z, direction)
    values = lax.psum(
        jnp.dot(kernel_tile, spread, precision=highest).astype(jnp.bfloat16), "ctr"
    ).astype(jnp.float32)
    back_part = lax.dot_general(kernel_tile, values, (((0,), (0,)), ((), ())), precision=highest)
    back = lax.psum(back_part, "pts")
    normal = back / total + ridge_weight * block_product(blocks, spread)
    image = block_product(current_z, normal)
    curve = lax.psum(jnp.sum(direction * image, axis=0), "ctr")
    step_size = norm_now / curve
    solution = step_size * direction
    residual = residual - step_size * image
    return (block_product(current_z, solution), residual)


def solution(mesh):
    in_specs = (P("pts", "ctr"), P("ctr", "pts"), P(), P("pts", "ctr"))
    out_specs = (P("ctr", None), P("ctr", None))
    return jax.shard_map(
        on_device, mesh=mesh, in_specs=in_specs, out_specs=out_specs, check_vma=False
    )
```

profile of v0, /device:TPU:64, one launch (start us, length us, event | category | flops | bytes accessed | tf_op | source)
XLA Modules:
  0.0 937.3 jit_solution(13510429586584781246)
XLA Ops:
  7.2 0.0 all-gather.9.cloned.1.call-start
  7.2 33.9 %all_gather.18 = bf16[512,256]{0,1:T(8,128)(2,1)S(1)} all-gather(bf16[512,8]{0,1:T(8,128)(2,1)} %param.5), channel_id=1, replica_groups=mesh['pts'=32,'ctr'=16] {'pts'}, dimensions={1}, use_global_device_ids=true | all-gather | bytes 270336 | tf_op jit(solution)/shard_map/all_gather | solution.py:29
  41.1 0.2 fusion.12
  41.3 0.5 fusion.3
  41.7 0.3 copy.6
  42.1 0.9 multiply_reduce_fusion
  43.7 0.2 broadcast_divide_fusion
  43.9 0.6 convolution_subtract_fusion.1
  44.5 1.6 convolution_multiply_fusion.4
  46.1 0.0 all-gather.9.cloned.1.call-update
  46.1 0.0 all-gather.7.cloned.1.call-start
  46.2 1.0 convolution_multiply_fusion.5
  47.1 0.0 all-gather.7.cloned.1.call-update
  47.2 0.0 copy-start.5
  47.2 0.0 all-reduce.5.cloned.1.call-start
  47.2 0.6 copy-done.7
  47.8 49.5 %all_gather.23 = bf16[256,128]{0,1:T(8,128)(2,1)S(1)} all-gather(bf16[256,8]{0,1:T(8,128)(2,1)S(1)} %copy-done.7), channel_id=1, replica_groups=mesh['pts'=32,'ctr'=16] {'ctr'}, dimensions={1}, use_global_device_ids=true | all-gather | bytes 69632 | tf_op jit(solution)/shard_map/all_gather | solution.py:27
  97.3 38.6 %all_gather.22 = bf16[256,256]{0,1:T(8,128)(2,1)S(1)} all-gather(bf16[256,16]{0,1:T(8,128)(2,1)S(1)} %copy-done.5), channel_id=1, replica_groups=mesh['pts'=32,'ctr'=16] {'ctr'}, dimensions={1}, use_global_device_ids=true | all-gather | bytes 139264 | tf_op jit(solution)/shard_map/all_gather | solution.py:26
  136.0 0.1 fusion.13
  136.1 0.4 fusion.6
  136.5 0.8 copy-done.1
  137.2 1.3 fusion.29
  138.5 0.0 all-reduce.5.cloned.1.call-update
  138.6 0.0 all-gather.11.cloned.1.call-start
  138.6 0.0 all-gather.9.cloned.1.call-done
  138.6 42.3 %all-gather.7.cloned.1.call-done = f32[512,512]{0,1:T(8,128)} async-done(((f32[512,16]{0,1:T(8,128)}), f32[512,512]{0,1:T(8,128)}) %all-gather.7.cloned.1.call-update) | async-done | bytes 1048592 | tf_op jit(solution)/shard_map/all_gather | solution.py:69
  180.9 2.0 convolution_subtract_fusion
  182.9 1.3 convolution_multiply_fusion.3
  184.2 0.0 all-gather.11.cloned.1.call-update
  184.2 0.0 all-reduce.7.cloned.1.call-start
  184.3 229.5 %all-reduce.5.cloned.1.call-done = f32[512,128]{1,0:T(8,128)} async-done(((f32[512,128]{1,0:T(8,128)}), f32[512,128]{1,0:T(8,128)}) %all-reduce.5.cloned.1.call-update) | async-done | bytes 262160 | tf_op jit(solution)/shard_map/psum | solution.py:77
  413.8 67.1 %all-gather.11.cloned.1.call-done = f32[512,512]{0,1:T(8,128)} async-done(((f32[512,16]{0,1:T(8,128)}), f32[512,512]{0,1:T(8,128)}) %all-gather.11.cloned.1.call-update) | async-done | bytes 1048592 | tf_op jit(solution)/shard_map/all_gather | solution.py:72
  480.9 3.2 fusion.17
  484.1 1.8 fusion.30
  485.9 0.0 copy-start.4
  485.9 0.7 copy-done.4
  486.6 1.2 convolution_convert_fusion
  487.8 0.0 all-reduce.7.cloned.1.call-update
  487.8 0.2 all-reduce.9.cloned.1.call-start
  488.1 160.2 %all-reduce.7.cloned.1.call-done = bf16[256,128]{1,0:T(8,128)(2,1)} async-done(((bf16[256,128]{1,0:T(8,128)(2,1)}), bf16[256,128]{1,0:T(8,128)(2,1)}) %all-reduce.7.cloned.1.call-update) | async-done | bytes 65552 | tf_op jit(solution)/shard_map/psum | solution.py:83
  648.2 2.4 fusion.31
  650.6 0.0 all-reduce.9.cloned.1.call-update
  650.6 227.8 %all-reduce.9.cloned.1.call-done = f32[512,128]{1,0:T(8,128)} async-done(((f32[512,128]{1,0:T(8,128)}), f32[512,128]{1,0:T(8,128)}) %all-reduce.9.cloned.1.call-update) | async-done | bytes 262160 | tf_op jit(solution)/shard_map/psum | solution.py:87
  878.4 2.0 fusion.7
  880.4 1.8 multiply_reduce_fusion.1
  882.2 44.9 %all-reduce = (f32[128]{0:T(128)S(1)}, f32[128]{0:T(128)S(1)}) all-reduce(f32[128]{0:T(128)S(1)} %get-tuple-element.3, f32[128]{0:T(128)S(1)} %get-tuple-element.2), channel_id=1, replica_groups=mesh['pts'=32,'ctr'=16] {'ctr'}, use_global_device_ids=true, to_apply=%region_5.6 | all-reduce | flops 256 | bytes 2048 | tf_op jit(solution)/shard_map/psum | solution.py:81
  927.2 0.7 multiply_subtract_fusion
  927.9 2.5 fusion.15
  (13 shorter events, 0.0 us)
Async XLA Ops:
  7.2 131.5 %all-gather.9.cloned.1.call-start = ((), (), s32[]{:S(2)}) async-start(), calls=%async_computation.4 | async-start | bytes 1081344 | tf_op jit(solution)/shard_map/all_gather | solution.py:68
  7.2 33.9 %copy-start.6 = (f32[256]{0:T(256)S(1)}, f32[256]{0:T(256)}, u32[]{:S(2)}) copy-start(f32[256]{0:T(256)} %param.6) | copy-start | bytes 3076
  46.1 134.8 %all-gather.7.cloned.1.call-start = ((), (), s32[]{:S(2)}) async-start(), calls=%async_computation.3 | async-start | bytes 1081344 | tf_op jit(solution)/shard_map/all_gather | solution.py:69
  47.1 0.7 copy-start.7
  47.2 50.2 %copy-start.5 = (bf16[256,16]{0,1:T(8,128)(2,1)S(1)}, bf16[256,16]{0,1:T(8,128)(2,1)}, u32[]{:S(2)}) copy-start(bf16[256,16]{0,1:T(8,128)(2,1)} %param.4) | copy-start | bytes 24580
  47.2 366.6 %all-reduce.5.cloned.1.call-start = ((), (), s32[]{:S(2)}) async-start(), calls=%async_computation | async-start | bytes 524288 | tf_op jit(solution)/shard_map/psum | solution.py:77
  136.4 0.8 copy-start.1
  138.6 342.3 %all-gather.11.cloned.1.call-start = ((), (), s32[]{:S(2)}) async-start(), calls=%async_computation.5 | async-start | bytes 1081344 | tf_op jit(solution)/shard_map/all_gather | solution.py:72
  180.9 2.0 copy-start.3
  184.2 464.0 %all-reduce.7.cloned.1.call-start = ((), (), s32[]{:S(2)}) async-start(), calls=%async_computation.1 | async-start | bytes 131072 | tf_op jit(solution)/shard_map/psum | solution.py:83
  480.9 3.2 copy-start
  484.1 2.5 copy-start.2
  485.9 0.7 copy-start.4
  487.8 390.5 %all-reduce.9.cloned.1.call-start = ((), (), s32[]{:S(2)}) async-start(), calls=%async_computation.2 | async-start | bytes 524288 | tf_op jit(solution)/shard_map/psum | solution.py:87
Sparse Core Ops, SparseCore 0:
  46.2 65.9 all-gather.8
  114.9 65.9 all-gather.6
  184.4 229.2 all-reduce.4
  416.3 64.5 all-gather.10
  488.0 160.2 all-reduce.6
  651.5 226.7 all-reduce.8
where the time goes:
time: 938 us; the launch traced here: 937 us
  waiting for transfers between devices  727 us (78%)
  blocking collectives  167 us (18%)
  matrix products  23.4 us (2%)
  between operations  15 us (2%)
    psum x1, waiting for transfers between devices, on_device(): right = lax.psum(right_part, 'pts') / math.sqrt(total)  229 us
    psum x1, waiting for transfers between devices, on_device(): back = lax.psum(back_part, 'pts')  228 us
    psum x1, waiting for transfers between devices, on_device(): lax.psum(jnp.dot(kernel_tile, spread, precision=highest).astype(jnp.bfloa...  160 us
    all_gather x1, waiting for transfers between devices, on_device(): current_z = lax.all_gather(next_z, 'pts', axis=2, tiled=True)  67.1 us
    all_gather x1, blocking collectives, on_device(): lax.all_gather(targets, 'ctr', axis=1, tiled=True)  49.5 us
    psum x1, blocking collectives, on_device(): norm_now = lax.psum(jnp.sum(residual * residual, axis=0), 'ctr')  44.9 us
    all_gather x1, waiting for transfers between devices, on_device(): lax.all_gather(next_z, 'pts', axis=2, tiled=True)  42.3 us
    all_gather x1, blocking collectives, on_device(): lax.all_gather(points, 'ctr', axis=1, tiled=True)  38.6 us
  transfers between devices with their start and end apart: 6, of which 5 were waited for; matrix products, arithmetic and copies ran while one was open for 1% of the time, Pallas kernels for 0%

commit v1 on v0

--- a/solution.py
+++ b/solution.py
@@ -84,7 +84,7 @@
         jnp.dot(kernel_tile, spread, precision=highest).astype(jnp.bfloat16), "ctr"
     ).astype(jnp.float32)
     back_part = lax.dot_general(kernel_tile, values, (((0,), (0,)), ((), ())), precision=highest)
-    back = lax.psum(back_part, "pts")
+    back = jnp.sum(lax.all_gather(back_part, axis_name="pts"), 0)
     normal = back / total + ridge_weight * block_product(blocks, spread)
     image = block_product(current_z, normal)
     curve = lax.psum(jnp.sum(direction * image, axis=0), "ctr")

time: 938 us -> 790 us (0.84)
  the two profiles are of different devices: /device:TPU:64 before, /device:TPU:16 now
where the time goes in v1:
time: 790 us
  waiting for transfers between devices  571 us (72%)
  blocking collectives  166 us (21%)
  matrix products  27.4 us (3%)
  between operations  14.9 us (2%)
    psum x1, waiting for transfers between devices, on_device(): right = lax.psum(right_part, 'pts') / math.sqrt(total)  223 us
    psum x1, waiting for transfers between devices, on_device(): lax.psum(jnp.dot(kernel_tile, spread, precision=highest).astype(jnp.bfloa...  160 us
    all_gather x1, waiting for transfers between devices, on_device(): current_z = lax.all_gather(next_z, 'pts', axis=2, tiled=True)  72.7 us
    all_gather x1, waiting for transfers between devices, on_device(): back = jnp.sum(lax.all_gather(back_part, axis_name='pts'), 0)  71.9 us
    all_gather x1, blocking collectives, on_device(): lax.all_gather(targets, 'ctr', axis=1, tiled=True)  48.5 us
    psum x1, blocking collectives, on_device(): norm_now = lax.psum(jnp.sum(residual * residual, axis=0), 'ctr')  45.7 us
    all_gather x1, waiting for transfers between devices, on_device(): lax.all_gather(next_y, 'pts', axis=2, tiled=True)  43.7 us
    all_gather x1, blocking collectives, on_device(): lax.all_gather(points, 'ctr', axis=1, tiled=True)  38.7 us
  transfers between devices with their start and end apart: 6, of which 5 were waited for; matrix products, arithmetic and copies ran while one was open for 1% of the time, Pallas kernels for 0%

profile of v1, /device:TPU:16, one launch (start us, length us, event | category | flops | bytes accessed | tf_op | source)
XLA Modules:
  0.0 789.7 jit_solution(16747300340248054417)
XLA Ops:
  7.2 0.0 copy-start.4
  7.2 0.0 all-gather.9.cloned.1.call-start
  7.3 33.5 %all_gather.24 = bf16[512,256]{0,1:T(8,128)(2,1)S(1)} all-gather(bf16[512,8]{0,1:T(8,128)(2,1)} %param.5), channel_id=1, replica_groups=mesh['pts'=32,'ctr'=16] {'pts'}, dimensions={1}, use_global_device_ids=true | all-gather | bytes 270336 | tf_op jit(solution)/shard_map/all_gather | solution.py:29
  40.8 0.8 fusion.12
  41.6 1.1 fusion.3
  42.7 0.3 copy.6
  43.1 0.9 multiply_reduce_fusion
  44.7 0.2 broadcast_divide_fusion
  45.0 0.6 convolution_subtract_fusion.1
  45.5 1.0 convolution_multiply_fusion.5
  46.5 0.0 all-gather.9.cloned.1.call-update
  46.5 0.0 all-gather.11.cloned.1.call-start
  46.6 1.6 convolution_multiply_fusion.4
  48.2 0.0 all-gather.11.cloned.1.call-update
  48.2 0.0 all-reduce.4.cloned.1.call-start
  48.2 48.5 %all_gather.29 = bf16[256,128]{0,1:T(8,128)(2,1)S(1)} all-gather(bf16[256,8]{0,1:T(8,128)(2,1)S(1)} %copy-done.5), channel_id=1, replica_groups=mesh['pts'=32,'ctr'=16] {'ctr'}, dimensions={1}, use_global_device_ids=true | all-gather | bytes 69632 | tf_op jit(solution)/shard_map/all_gather | solution.py:27
  96.7 38.7 %all_gather.28 = bf16[256,256]{0,1:T(8,128)(2,1)S(1)} all-gather(bf16[256,16]{0,1:T(8,128)(2,1)S(1)} %copy-done.3), channel_id=1, replica_groups=mesh['pts'=32,'ctr'=16] {'ctr'}, dimensions={1}, use_global_device_ids=true | all-gather | bytes 139264 | tf_op jit(solution)/shard_map/all_gather | solution.py:26
  135.4 0.1 fusion.13
  135.6 0.3 fusion.6
  135.9 0.8 copy-done.1
  136.7 1.3 fusion.29
  138.0 0.0 all-reduce.4.cloned.1.call-update
  138.0 0.0 all-gather.13.cloned.1.call-start
  138.1 0.0 all-gather.9.cloned.1.call-done
  138.1 43.7 %all-gather.11.cloned.1.call-done = f32[512,512]{0,1:T(8,128)} async-done(((f32[512,16]{0,1:T(8,128)}), f32[512,512]{0,1:T(8,128)}) %all-gather.11.cloned.1.call-update) | async-done | bytes 1048592 | tf_op jit(solution)/shard_map/all_gather | solution.py:68
  181.9 1.9 convolution_subtract_fusion
  183.7 2.5 convolution_multiply_fusion.3
  186.2 0.0 all-gather.13.cloned.1.call-update
  186.3 0.0 all-reduce.6.cloned.1.call-start
  186.3 222.8 %all-reduce.4.cloned.1.call-done = f32[512,128]{1,0:T(8,128)} async-done(((f32[512,128]{1,0:T(8,128)}), f32[512,128]{1,0:T(8,128)}) %all-reduce.4.cloned.1.call-update) | async-done | bytes 262160 | tf_op jit(solution)/shard_map/psum | solution.py:77
  409.1 72.7 %all-gather.13.cloned.1.call-done = f32[512,512]{0,1:T(8,128)} async-done(((f32[512,16]{0,1:T(8,128)}), f32[512,512]{0,1:T(8,128)}) %all-gather.13.cloned.1.call-update) | async-done | bytes 1048592 | tf_op jit(solution)/shard_map/all_gather | solution.py:72
  481.8 3.2 fusion.17
  485.0 3.0 fusion.30
  488.0 0.0 copy-start.2
  488.0 0.7 copy-done.2
  488.7 2.3 convolution_convert_fusion
  491.0 0.0 all-reduce.6.cloned.1.call-update
  491.0 0.2 all-gather.15.cloned.1.call-start
  491.2 159.9 %all-reduce.6.cloned.1.call-done = bf16[256,128]{1,0:T(8,128)(2,1)} async-done(((bf16[256,128]{1,0:T(8,128)(2,1)}), bf16[256,128]{1,0:T(8,128)(2,1)}) %all-reduce.6.cloned.1.call-update) | async-done | bytes 65552 | tf_op jit(solution)/shard_map/psum | solution.py:83
  651.2 2.4 fusion.31
  653.5 0.0 all-gather.15.cloned.1.call-update
  653.6 71.9 %all-gather.15.cloned.1.call-done = f32[16384,128]{1,0:T(8,128)} async-done(((f32[512,128]{1,0:T(8,128)}), f32[16384,128]{1,0:T(8,128)}) %all-gather.15.cloned.1.call-update) | async-done | bytes 8388624 | tf_op jit(solution)/shard_map/all_gather | solution.py:87
  725.5 4.5 reduce_sum.58
  730.0 2.0 fusion.7
  732.0 1.8 multiply_reduce_fusion.1
  733.8 45.7 %all-reduce = (f32[128]{0:T(128)S(1)}, f32[128]{0:T(128)S(1)}) all-reduce(f32[128]{0:T(128)S(1)} %get-tuple-element.3, f32[128]{0:T(128)S(1)} %get-tuple-element.2), channel_id=1, replica_groups=mesh['pts'=32,'ctr'=16] {'ctr'}, use_global_device_ids=true, to_apply=%region_5.6 | all-reduce | flops 256 | bytes 2048 | tf_op jit(solution)/shard_map/psum | solution.py:81
  779.6 0.7 multiply_subtract_fusion
  780.3 2.5 fusion.15
  (10 shorter events, 0.0 us)
Async XLA Ops:
  7.2 128.3 %copy-start.4 = (f32[256]{0:T(256)S(1)}, f32[256]{0:T(256)}, u32[]{:S(2)}) copy-start(f32[256]{0:T(256)} %param.6) | copy-start | bytes 3076
  7.2 41.1 %copy-start.5 = (bf16[256,8]{0,1:T(8,128)(2,1)S(1)}, bf16[256,8]{0,1:T(8,128)(2,1)}, u32[]{:S(2)}) copy-start(bf16[256,8]{0,1:T(8,128)(2,1)} %param.7) | copy-start | bytes 12292
  7.2 89.6 %copy-start.3 = (bf16[256,16]{0,1:T(8,128)(2,1)S(1)}, bf16[256,16]{0,1:T(8,128)(2,1)}, u32[]{:S(2)}) copy-start(bf16[256,16]{0,1:T(8,128)(2,1)} %param.4) | copy-start | bytes 24580
  7.2 130.9 %all-gather.9.cloned.1.call-start = ((), (), s32[]{:S(2)}) async-start(), calls=%async_computation.2 | async-start | bytes 1081344 | tf_op jit(solution)/shard_map/all_gather | solution.py:69
  46.5 135.4 %all-gather.11.cloned.1.call-start = ((), (), s32[]{:S(2)}) async-start(), calls=%async_computation.3 | async-start | bytes 1081344 | tf_op jit(solution)/shard_map/all_gather | solution.py:68
  48.2 361.0 %all-reduce.4.cloned.1.call-start = ((), (), s32[]{:S(2)}) async-start(), calls=%async_computation | async-start | bytes 524288 | tf_op jit(solution)/shard_map/psum | solution.py:77
  135.9 0.8 copy-start.1
  138.0 343.8 %all-gather.13.cloned.1.call-start = ((), (), s32[]{:S(2)}) async-start(), calls=%async_computation.4 | async-start | bytes 1081344 | tf_op jit(solution)/shard_map/all_gather | solution.py:72
  186.3 464.9 %all-reduce.6.cloned.1.call-start = ((), (), s32[]{:S(2)}) async-start(), calls=%async_computation.1 | async-start | bytes 131072 | tf_op jit(solution)/shard_map/psum | solution.py:83
  481.8 250.2 %copy-start = (f32[512,512]{0,1:T(8,128)S(1)}, f32[512,512]{0,1:T(8,128)}, u32[]{:S(2)}) copy-start(f32[512,512]{0,1:T(8,128)} %all-gather.13.cloned.1.call-done) | copy-start | bytes 3145732
  488.0 0.7 copy-start.2
  491.0 234.5 %all-gather.15.cloned.1.call-start = ((), (), s32[]{:S(2)}) async-start(), calls=%async_computation.5 | async-start | bytes 8650752 | tf_op jit(solution)/shard_map/all_gather | solution.py:87
Sparse Core Ops, SparseCore 0:
  46.6 67.1 all-gather.8
  115.9 65.8 all-gather.10
  185.3 223.7 all-reduce.3
  411.7 70.0 all-gather.12
  491.1 160.0 all-reduce.5
  653.7 71.6 all-gather.14
